TPU v7x, 256 devices: a whole 4x4x8 slice. The times are simulated.
256 devices in a mesh: row: 4 (over z_lo, core), col: 64 (over y, z_hi, x).
Axes of the slice: x: 4, y: 4, z: 8 (z_hi: 4, z_lo: 2; z = z_hi * 2 + z_lo), core: 2. Of those that a mesh axis runs over, the one named last changes fastest.
Arguments:
- tokens: bfloat16 [1024, 8192], P('col', 'row'), may hold values from -6 to 6
- out_grad: bfloat16 [1024, 8192], P('col', 'row'), may hold values from -2 to 2
- gate_weight: bfloat16 [8192, 28672], P('row', 'col'), may hold values from -0.0625 to 0.0625
- up_weight: bfloat16 [8192, 28672], P('row', 'col'), may hold values from -0.0625 to 0.0625
- down_weight: bfloat16 [28672, 8192], P('col', 'row'), may hold values from -0.03125 to 0.03125
Outputs:
- grad_input: bfloat16 [1024, 8192], P('col', 'row')
- grad_gate: bfloat16 [8192, 28672], P('row', 'col')
- grad_up: bfloat16 [8192, 28672], P('row', 'col')
- grad_down: bfloat16 [28672, 8192], P('col', 'row')
All inputs are finite; a program needn't handle non-finite values.
Results may differ from a plain program's by a relative error of at most 0.005.
Values may be sent and summed in bfloat16 or wider, within the bound.
No kernel may reach another device: no remote copies, remote signals or barrier semaphores. Data moves between devices by JAX's collectives and lax.ppermute only.
A program may use at most 128 MiB of HBM per device.

v0:
```python
import jax
import jax.numpy as jnp
from jax import lax
from jax.sharding import PartitionSpec as P


def pointwise(gate, up, hidden_grad):
    logistic = jax.nn.sigmoid(gate)
    active = gate * logistic
    hidden = (active * up).astype(jnp.bfloat16)
    d_gate = (hidden_grad * up * logistic * (1.0 + gate * (1.0 - logistic))).astype(jnp.bfloat16)
    d_up = (hidden_grad * active).astype(jnp.bfloat16)
    return (hidden, d_gate, d_up)


def contract_last(left, right):
    return lax.dot_general(
        left, right, (((1,), (1,)), ((), ())), preferred_element_type=jnp.float32
    )


def contract_first(left, right):
    return lax.dot_general(
        left, right, (((0,), (0,)), ((), ())), preferred_element_type=jnp.float32
    )


def local(tokens, out_grad, gate_weight, up_weight, down_weight):
    full_tokens, full_grad = (
        lax.all_gather(tokens, "col", axis=0, tiled=True),
        lax.all_gather(out_grad, "col", axis=0, tiled=True),
    )
    gate_part = jnp.dot(full_tokens, gate_weight, preferred_element_type=jnp.float32)
    up_part = jnp.dot(full_tokens, up_weight, preferred_element_type=jnp.float32)
    hidden_part = contract_last(full_grad, down_weight)
    gate, up, hidden_grad = lax.psum((gate_part, up_part, hidden_part), "row")
    hidden, d_gate, d_up = pointwise(gate, up, hidden_grad)
    grad_down = contract_first(hidden, full_grad).astype(jnp.bfloat16)
    grad_gate = contract_first(full_tokens, d_gate).astype(jnp.bfloat16)
    grad_up = contract_first(full_tokens, d_up).astype(jnp.bfloat16)
    grad_input = lax.psum_scatter(
        contract_last(d_gate, gate_weight) + contract_last(d_up, up_weight),
        "col",
        scatter_dimension=0,
        tiled=True,
    ).astype(jnp.bfloat16)
    return (grad_input, grad_gate, grad_up, grad_down)


def solution(mesh):
    in_specs = (P("col", "row"), P("col", "row"), P("row", "col"), P("row", "col"), P("col", "row"))
    out_specs = (P("col", "row"), P("row", "col"), P("row", "col"), P("col", "row"))
    return jax.shard_map(local, mesh=mesh, in_specs=in_specs, out_specs=out_specs, check_vma=False)
```

profile of v0, /device:TPU:0, one launch (start us, length us, event | category | flops | bytes accessed | tf_op | source)
XLA Modules:
  0.0 743.4 jit_solution(6476649636383026013)
XLA Ops:
  7.2 0.0 copy-start
  7.2 0.0 all-gather.5.cloned.1.call-start
  7.2 0.7 all-gather.5.cloned.1.call-update
  7.9 0.0 all-gather.3.cloned.1.call-start
  8.0 0.7 all-gather.3.cloned.1.call-update
  8.7 0.0 all-reduce.3.cloned.1.call-start
  8.7 93.1 %all-gather.5.cloned.1.call-done = bf16[1024,2048]{1,0:T(8,128)(2,1)} async-done(((bf16[16,2048]{1,0:T(8,128)(2,1)}), bf16[1024,2048]{1,0:T(8,128)(2,1)}) %all-gather.5.cloned.1.call-update) | async-done | bytes 4194320 | tf_op jit(solution)/shard_map/all_gather | solution.py:30
  101.8 0.0 copy-done
  101.8 5.7 fusion.7
  107.4 0.0 copy-done.1
  107.4 0.0 copy-done.7
  107.4 3.3 fusion.6
  110.8 82.0 %all-gather.3.cloned.1.call-done = bf16[1024,2048]{1,0:T(8,128)(2,1)} async-done(((bf16[16,2048]{1,0:T(8,128)(2,1)}), bf16[1024,2048]{1,0:T(8,128)(2,1)}) %all-gather.3.cloned.1.call-update) | async-done | bytes 4194320 | tf_op jit(solution)/shard_map/all_gather | solution.py:31
  192.7 6.1 fusion.5
  198.8 0.0 all-reduce.3.cloned.1.call-update
  198.9 0.2 reduce-scatter.2.cloned.1.call-start
  199.1 116.1 %all-reduce.3.cloned.1.call-done = (f32[1024,448]{0,1:T(8,128)}, f32[1024,448]{0,1:T(8,128)}, f32[1024,448]{0,1:T(8,128)}) async-done(((f32[1024,448]{0,1:T(8,128)}, f32[1024,448]{0,1:T(8,128)}, f32[1024,448]{0,1:T(8,128)}), (f32[1024,448]{0,1:T(8,128)}, f32[1024,448]{0,1:T(8,128)}, f32[1024,448]{0,1:T(8,128)})) %all-reduce.3.cloned.1.call-update) | async-done | bytes 5505040 | tf_op jit(solution)/shard_map/psum | solution.py:36
  315.2 3.7 multiply_convert_fusion.1
  318.9 0.0 copy-start.5
  318.9 0.0 copy-start.2
  318.9 2.4 fusion.8
  321.3 0.0 copy-done.5
  321.4 5.9 convolution_add_fusion
  327.3 0.0 reduce-scatter.2.cloned.1.call-update
  327.3 0.0 copy-start.6
  327.3 5.6 fusion.1
  333.0 3.3 fusion
  336.3 0.0 copy-done.3
  336.3 0.3 copy-done.9
  336.6 3.4 convolution_convert_fusion
  340.0 395.3 %reduce-scatter.2.cloned.1.call-done = f32[16,2048]{1,0:T(8,128)} async-done(((f32[1024,2048]{1,0:T(8,128)}), f32[16,2048]{1,0:T(8,128)}) %reduce-scatter.2.cloned.1.call-update) | async-done | bytes 131088 | tf_op jit(solution)/shard_map/reduce_scatter | solution.py:41
  735.3 1.5 convert_element_type.29
  (10 shorter events, 0.0 us)
Async XLA Ops:
  7.2 94.6 %copy-start = (bf16[2048,448]{0,1:T(8,128)(2,1)S(1)}, bf16[2048,448]{0,1:T(8,128)(2,1)}, u32[]{:S(2)}) copy-start(bf16[2048,448]{0,1:T(8,128)(2,1)} %param.7) | copy-start | bytes 5505028
  7.2 94.6 %all-gather.5.cloned.1.call-start = ((), (), s32[]{:S(2)}) async-start(), calls=%async_computation.2 | async-start | bytes 4259840 | tf_op jit(solution)/shard_map/all_gather | solution.py:30
  7.9 184.8 %all-gather.3.cloned.1.call-start = ((), (), s32[]{:S(2)}) async-start(), calls=%async_computation.1 | async-start | bytes 4259840 | tf_op jit(solution)/shard_map/all_gather | solution.py:31
  8.7 306.5 %all-reduce.3.cloned.1.call-start = ((), (), s32[]{:S(2)}) async-start(), calls=%async_computation.4 | async-start | bytes 11010048 | tf_op jit(solution)/shard_map/psum | solution.py:36
  101.8 5.7 copy-start.1
  101.8 5.7 copy-start.7
  198.9 536.4 %reduce-scatter.2.cloned.1.call-start = ((), (), s32[]{:S(2)}) async-start(), calls=%async_computation.3 | async-start | bytes 8519680 | tf_op jit(solution)/shard_map/reduce_scatter | solution.py:41
  318.9 2.4 copy-start.5
  318.9 2.4 copy-start.2
  327.3 5.7 copy-start.6
  327.3 5.7 copy-start.8
  332.9 3.4 copy-start.3
  332.9 3.4 copy-start.4
  333.0 3.7 copy-start.9
Sparse Core Ops, SparseCore 0:
  11.3 90.3 all-gather.4
  105.1 87.6 all-gather.2
  199.0 116.1 all-reduce.2
  327.4 407.8 reduce-scatter.1
where the time goes:
time: 743 us
  waiting for transfers between devices  688 us (93%)
  matrix products  35.7 us (5%)
  between operations  13.8 us (2%)
    reduce_scatter x1, waiting for transfers between devices, local(): lax.psum_scatter(contract_last(d_gate, gate_weight) + contract_last(d_up,...  395 us
    psum x1, waiting for transfers between devices, local(): gate, up, hidden_grad = lax.psum((gate_part, up_part, hidden_part), 'row')  116 us
    all_gather x1, waiting for transfers between devices, local(): lax.all_gather(tokens, 'col', axis=0, tiled=True)  93.1 us
    all_gather x1, waiting for transfers between devices, local(): lax.all_gather(out_grad, 'col', axis=0, tiled=True)  82 us
  transfers between devices with their start and end apart: 4, of which 4 were waited for; matrix products, arithmetic and copies ran while one was open for 3% of the time, Pallas kernels for 0%

commit v1 on v0

--- a/solution.py
+++ b/solution.py
@@ -2,6 +2,14 @@
 import jax.numpy as jnp
 from jax import lax
 from jax.sharding import PartitionSpec as P
+
+
+def pair_the_figure(arr_in, mesh_dim="col"):
+    tall = jax.lax.axis_size(mesh_dim)
+    prior = jnp.stack(tall * [arr_in])
+    part_next = jax.lax.all_to_all(prior, axis_name=mesh_dim, split_axis=0, concat_axis=0)
+    u1 = jnp.concatenate(part_next, axis=0)
+    return u1
 
 
 def pointwise(gate, up, hidden_grad):
@@ -28,7 +36,7 @@
 def local(tokens, out_grad, gate_weight, up_weight, down_weight):
     full_tokens, full_grad = (
         lax.all_gather(tokens, "col", axis=0, tiled=True),
-        lax.all_gather(out_grad, "col", axis=0, tiled=True),
+        pair_the_figure(out_grad),
     )
     gate_part = jnp.dot(full_tokens, gate_weight, preferred_element_type=jnp.float32)
     up_part = jnp.dot(full_tokens, up_weight, preferred_element_type=jnp.float32)

time: 743 us -> 701 us (0.943)
  waiting for transfers between devices: 688 us -> 627 us
  starting transfers between devices: 0.34 us -> 13.4 us
    all_to_all x0 -> x1, waiting for transfers between devices: none -> 110 us  [pair_the_figure(): jax.lax.all_to_all(prior, axis_name=mesh_dim, split_axis=0, concat_axis=0)]
    all_gather x1, waiting for transfers between devices: 93.1 us -> 6.32 us  [local(): lax.all_gather(tokens, 'col', axis=0, tiled=True)]
    all_gather x1 -> x0, waiting for transfers between devices: 82 us -> none  [local(): lax.all_gather(out_grad, 'col', axis=0, tiled=True)]
    all_to_all x0 -> x1, starting transfers between devices: none -> 13.1 us  [pair_the_figure(): jax.lax.all_to_all(prior, axis_name=mesh_dim, split_axis=0, concat_axis=0)]
where the time goes in v1:
time: 701 us
  waiting for transfers between devices  627 us (89%)
  matrix products  38 us (5%)
  between operations  13.8 us (2%)
  starting transfers between devices  13.4 us (2%)
    reduce_scatter x1, waiting for transfers between devices, local(): lax.psum_scatter(contract_last(d_gate, gate_weight) + contract_last(d_up,...  393 us
    psum x1, waiting for transfers between devices, local(): gate, up, hidden_grad = lax.psum((gate_part, up_part, hidden_part), 'row')  117 us
    all_to_all x1, waiting for transfers between devices, pair_the_figure(): jax.lax.all_to_all(prior, axis_name=mesh_dim, split_axis=0, concat_axis=0)  110 us
    dot_general x3, matrix products, contract_first(): lax.dot_general(left, right, (((0,), (0,)), ((), ())), preferred_element_...  14.6 us
    dot_general x3, matrix products, contract_last(): lax.dot_general(left, right, (((1,), (1,)), ((), ())), preferred_element_...  14.5 us
  transfers between devices with their start and end apart: 4, of which 4 were waited for; matrix products, arithmetic and copies ran while one was open for 3% of the time, Pallas kernels for 0%

profile of v1, /device:TPU:0, one launch (start us, length us, event | category | flops | bytes accessed | tf_op | source)
XLA Modules:
  0.0 700.8 jit_solution(7238394680840896660)
XLA Ops:
  7.2 0.0 copy-start
  7.2 3.5 stack.2
  10.6 13.1 %all-to-all-start = ((bf16[64,16,2048]{2,1,0:T(8,128)(2,1)}), bf16[64,16,2048]{2,1,0:T(8,128)(2,1)}, u32[]{:S(2)}, u32[]{:S(2)}) async-start(bf16[64,16,2048]{2,1,0:T(8,128)(2,1)} %stack.2), calls=%async_computation | async-start | bytes 8388608 | tf_op jit(solution)/shard_map/all_to_all | solution.py:10
  23.7 0.0 all-gather.2.cloned.1.call-start
  23.8 0.7 all-gather.2.cloned.1.call-update
  24.5 0.0 all-reduce.3.cloned.1.call-start
  24.5 109.7 %all-to-all-done = bf16[64,16,2048]{2,1,0:T(8,128)(2,1)} async-done(((bf16[64,16,2048]{2,1,0:T(8,128)(2,1)}), bf16[64,16,2048]{2,1,0:T(8,128)(2,1)}, u32[]{:S(2)}, u32[]{:S(2)}) %all-to-all-start) | async-done | bytes 4194336 | tf_op jit(solution)/shard_map/all_to_all | solution.py:10
  134.2 6.2 fusion.5
  140.4 6.3 all-gather.2.cloned.1.call-done
  146.7 0.0 copy-done
  146.8 5.7 fusion.7
  152.4 0.0 copy-done.1
  152.4 0.0 copy-done.7
  152.4 3.3 fusion.6
  155.7 0.0 all-reduce.3.cloned.1.call-update
  155.8 0.2 reduce-scatter.2.cloned.1.call-start
  156.0 117.3 %all-reduce.3.cloned.1.call-done = (f32[1024,448]{0,1:T(8,128)}, f32[1024,448]{0,1:T(8,128)}, f32[1024,448]{0,1:T(8,128)}) async-done(((f32[1024,448]{0,1:T(8,128)}, f32[1024,448]{0,1:T(8,128)}, f32[1024,448]{0,1:T(8,128)}), (f32[1024,448]{0,1:T(8,128)}, f32[1024,448]{0,1:T(8,128)}, f32[1024,448]{0,1:T(8,128)})) %all-reduce.3.cloned.1.call-update) | async-done | bytes 5505040 | tf_op jit(solution)/shard_map/psum | solution.py:44
  273.3 3.7 multiply_convert_fusion.1
  277.0 0.0 copy-start.5
  277.0 0.0 copy-start.2
  277.0 2.4 fusion.8
  279.4 0.0 copy-done.5
  279.4 0.0 copy-done.2
  279.4 5.9 convolution_add_fusion
  285.3 0.0 reduce-scatter.2.cloned.1.call-update
  285.3 0.0 copy-start.6
  285.3 0.0 copy-start.8
  285.3 5.6 fusion.1
  291.0 3.3 fusion
  294.3 5.6 convolution_convert_fusion
  299.9 392.8 %reduce-scatter.2.cloned.1.call-done = f32[16,2048]{1,0:T(8,128)} async-done(((f32[1024,2048]{1,0:T(8,128)}), f32[16,2048]{1,0:T(8,128)}) %reduce-scatter.2.cloned.1.call-update) | async-done | bytes 131088 | tf_op jit(solution)/shard_map/reduce_scatter | solution.py:49
  692.7 1.5 convert_element_type.29
  (8 shorter events, 0.0 us)
Async XLA Ops:
  7.2 139.6 %copy-start = (bf16[2048,448]{0,1:T(8,128)(2,1)S(1)}, bf16[2048,448]{0,1:T(8,128)(2,1)}, u32[]{:S(2)}) copy-start(bf16[2048,448]{0,1:T(8,128)(2,1)} %param.7) | copy-start | bytes 5505028
  10.6 123.6 %all-to-all-start = ((bf16[64,16,2048]{2,1,0:T(8,128)(2,1)}), bf16[64,16,2048]{2,1,0:T(8,128)(2,1)}, u32[]{:S(2)}, u32[]{:S(2)}) async-start(bf16[64,16,2048]{2,1,0:T(8,128)(2,1)} %stack.2), calls=%async_computation | async-start | bytes 8388608 | tf_op jit(solution)/shard_map/all_to_all | solution.py:10
  23.7 123.0 %all-gather.2.cloned.1.call-start = ((), (), s32[]{:S(2)}) async-start(), calls=%async_computation.2 | async-start | bytes 4259840 | tf_op jit(solution)/shard_map/all_gather | solution.py:38
  24.5 248.8 %all-reduce.3.cloned.1.call-start = ((), (), s32[]{:S(2)}) async-start(), calls=%async_computation.4 | async-start | bytes 11010048 | tf_op jit(solution)/shard_map/psum | solution.py:44
  146.7 5.7 copy-start.1
  146.7 5.7 copy-start.7
  155.8 537.0 %reduce-scatter.2.cloned.1.call-start = ((), (), s32[]{:S(2)}) async-start(), calls=%async_computation.3 | async-start | bytes 8519680 | tf_op jit(solution)/shard_map/reduce_scatter | solution.py:49
  277.0 2.4 copy-start.5
  277.0 2.4 copy-start.2
  285.3 5.7 copy-start.6
  285.3 5.7 copy-start.8
  291.0 3.3 copy-start.3
  291.0 3.3 copy-start.4
Sparse Core Ops, SparseCore 0:
  27.9 118.8 all-gather.1
  155.9 117.3 all-reduce.2
  285.4 407.2 reduce-scatter.1
